TPU v7x, 256 devices: a whole 4x4x8 slice. The times are simulated.
256 devices in a mesh: cfg: 2 (over core), req: 16 (over x_hi, z), seq: 8 (over x_lo, y).
Axes of the slice: x: 4 (x_hi: 2, x_lo: 2; x = x_hi * 2 + x_lo), y: 4, z: 8, core: 2. Of those that a mesh axis runs over, the one named last changes fastest.
Arguments:
- hidden: bfloat16 [2, 16, 2304, 1536], P('cfg', 'req', 'seq'), may hold values from -6 to 6
- latent: float32 [16, 2304, 64], P('req', 'seq', 'cfg'), may hold values from -6 to 6
- modulation: float32 [16, 5, 1536], P('req'), may hold values from -3 to 3
- w_qkv: bfloat16 [1536, 4608], P('req'), may hold values from -1 to 1
- w_out: bfloat16 [1536, 1536], P('req'), may hold values from -0.15625 to 0.15625
- q_gain: float32 [1536], replicated, may hold values from 0 to 2
- k_gain: float32 [1536], replicated, may hold values from 0 to 2
- w_head: bfloat16 [1536, 64], replicated, may hold values from -0.15625 to 0.15625
- lengths: int32 [16], P('req'), may hold values from 288 to 2304, as said below
- guidance: float32 [16], P('req'), may hold values from 3 to 7
- step_size: float32 [16], P('req'), may hold values from 0.03 to 0.3
Outputs:
- new_latent: float32 [16, 2304, 64], P('req', 'seq', 'cfg')
Inputs may be any that keep to these rules, and one draw needn't show every extreme that they name: `lengths`: some request has exactly 2304 video tokens in every draw.
All inputs are finite; a program needn't handle non-finite values.
Results may differ from a plain program's by a relative error of at most 0.01.
Values may be sent and summed in bfloat16 or wider, within the bound.
A program may use at most 128 MiB of HBM per device.

v0:
```python
import jax
import jax.numpy as jnp
from jax import lax
from jax.sharding import PartitionSpec as P

DH = 128


def passed_along(value, axis, steps):
    count = lax.axis_size(axis)
    pairs = [(source, (source + steps) % count) for source in range(count)]
    return lax.ppermute(value, axis, pairs)


def from_partner(value, axis, apart):
    mask = 2**apart
    pairs = [(source, source ^ mask) for source in range(lax.axis_size(axis))]
    return lax.ppermute(value, axis, pairs)


def layer_norm(values):
    centered = values - jnp.mean(values, axis=-1, keepdims=True)
    return centered / jnp.sqrt(jnp.mean(centered * centered, axis=-1, keepdims=True) + 1e-06)


def rms_gain(values, gain):
    return values / jnp.sqrt(jnp.mean(values * values, axis=-1, keepdims=True) + 1e-06) * gain


def add_rows(left, piece):
    return jnp.dot(left, piece, preferred_element_type=jnp.float32)


def attend(state, query, stacked, start, length):
    top, total, weighted = state
    keys = stacked[0]
    values = stacked[1]
    count = keys.shape[0]
    scores = jnp.einsum("qhd,khd->qhk", query, keys, preferred_element_type=jnp.float32) / jnp.sqrt(
        jnp.float32(query.shape[2])
    )
    valid = start + jnp.arange(count, dtype=jnp.int32) < length
    scores = jnp.where(valid[None, None, :], scores, jnp.float32(-1e30))
    new_top = jnp.maximum(top, jnp.max(scores, axis=-1))
    factor = jnp.exp(top - new_top)
    probs = jnp.where(valid[None, None, :], jnp.exp(scores - new_top[:, :, None]), jnp.float32(0.0))
    total = total * factor + jnp.sum(probs, axis=-1)
    weighted = weighted * factor[:, :, None] + jnp.einsum(
        "qhk,khd->qhd", probs.astype(jnp.bfloat16), values, preferred_element_type=jnp.float32
    )
    return (new_top, total, weighted)


def local(
    hidden, latent, modulation, w_qkv, w_out, q_gain, k_gain, w_head, lengths, guidance, step_size
):
    state = hidden[0, 0]
    modes = modulation[0]
    length = lengths[0]
    rows = state.shape[0]
    width = state.shape[1]
    heads = q_gain.shape[0] // DH
    wide = state.astype(jnp.float32)
    normed = (layer_norm(wide) * (1.0 + modes[1]) + modes[0]).astype(jnp.bfloat16)
    qkv = add_rows(normed, lax.all_gather(w_qkv, "req", axis=0, tiled=True))
    query = rms_gain(qkv[:, :width], q_gain).astype(jnp.bfloat16).reshape(rows, heads, DH)
    keys = rms_gain(qkv[:, width : 2 * width], k_gain).astype(jnp.bfloat16).reshape(rows, heads, DH)
    values = qkv[:, 2 * width :].astype(jnp.bfloat16).reshape(rows, heads, DH)
    stacked = jnp.stack([keys, values])
    position = lax.axis_index("seq")
    members = lax.axis_size("seq")
    start_state = (
        jnp.full((rows, heads), -1e30, jnp.float32),
        jnp.zeros((rows, heads), jnp.float32),
        jnp.zeros((rows, heads, DH), jnp.float32),
    )
    first = attend(start_state, query, stacked, position * rows, length)

    def cycle_step(turn, carry):
        moving, inner = carry
        moving = passed_along(moving, "seq", 1)
        source = (position - turn) % members
        return (moving, attend(inner, query, moving, source * rows, length))

    moved, result = lax.fori_loop(1, members, cycle_step, (stacked, first))
    top, total, weighted = result
    attended = (weighted / total[:, :, None]).reshape(rows, width).astype(jnp.bfloat16)
    projected = add_rows(attended, lax.all_gather(w_out, "req", axis=0, tiled=True))
    block_out = (wide + modes[2] * projected).astype(jnp.bfloat16)
    head_in = (layer_norm(block_out.astype(jnp.float32)) * (1.0 + modes[4]) + modes[3]).astype(
        jnp.bfloat16
    )
    velocity = jnp.dot(head_in, w_head, preferred_element_type=jnp.float32)
    branch = lax.axis_index("cfg")
    scale = guidance[0]
    channels = velocity.shape[1] // 2
    own = lax.dynamic_slice_in_dim(velocity, branch * channels, channels, 1)
    outgoing = lax.dynamic_slice_in_dim(velocity, (1 - branch) * channels, channels, 1)
    other = from_partner(outgoing.astype(jnp.bfloat16), "cfg", 0).astype(outgoing.dtype)
    cond = jnp.where(branch == 0, own, other)
    uncond = jnp.where(branch == 0, other, own)
    guided = uncond + scale * (cond - uncond)
    valid = position * rows + jnp.arange(rows, dtype=jnp.int32) < length
    current = latent[0]
    updated = jnp.where(valid[:, None], current - step_size[0] * guided, current)
    return updated[None]


def solution(mesh):
    return jax.shard_map(
        local,
        mesh=mesh,
        in_specs=(
            P("cfg", "req", "seq", None),
            P("req", "seq", "cfg"),
            P("req", None, None),
            P("req", None),
            P("req", None),
            P(),
            P(),
            P(),
            P("req"),
            P("req"),
            P("req"),
        ),
        out_specs=P("req", "seq", "cfg"),
        check_vma=False,
    )
```

profile of v0, /device:TPU:1, one launch (start us, length us, event | category | flops | bytes accessed | tf_op | source)
XLA Modules:
  0.0 648.4 jit_solution(9502393456810084686)
XLA Ops:
  10.2 198.2 %all-gather.3.cloned.1.call-done = bf16[1536,4608]{1,0:T(8,128)(2,1)} async-done(((bf16[96,4608]{1,0:T(8,128)(2,1)}), bf16[1536,4608]{1,0:T(8,128)(2,1)}) %all-gather.3.cloned.1.call-update) | async-done | bytes 14155792 | tf_op jit(solution)/shard_map/all_gather | solution.py:65
  208.3 7.9 %fusion.42 = f32[288,4608]{1,0:T(8,128)S(1)} fusion(bf16[1536,4608]{1,0:T(8,128)(2,1)} %all-gather.3.cloned.1.call-done, bf16[1,1,288,1536]{3,2,1,0:T(8,128)(2,1)S(1)} %copy-done.2, f32[1536]{0:T(1024)S(1)} %get-tuple-element.226, f32[1536]{0:T(1024)S(1)} %get-tuple-element.227, f32[288]{0:T(512)S(1)} %add_sqrt_fusion.3, f32[288]{0:T(512)S(1)} %broadcast_multiply_fusion.1), kind=kOutput, calls=%fused_computation.61 | convolution fusion | flops 4079517696 | bytes 20363520 | tf_op jit(solution)/shard_map/dot_general | solution.py:31
  216.7 1.9 copy-done.1
  218.6 1.5 fusion.56
  222.8 1.7 copy.25
  226.7 1.5 fusion.21
  228.2 5.1 bitcast_add_fusion.1
  233.3 75.5 %all-gather.5.cloned.1.call-done = bf16[1536,1536]{1,0:T(8,128)(2,1)} async-done(((bf16[96,1536]{1,0:T(8,128)(2,1)}), bf16[1536,1536]{1,0:T(8,128)(2,1)}) %all-gather.5.cloned.1.call-update) | async-done | bytes 4718608 | tf_op jit(solution)/shard_map/all_gather | solution.py:88
  308.7 315.1 %while.21 = (s32[]{:T(128)}, bf16[2,288,12,128]{3,1,2,0:T(8,128)(2,1)}, f32[288,12]{0,1:T(8,128)S(1)}, f32[288,12]{0,1:T(8,128)S(1)}, f32[288,12,128]{2,0,1:T(8,...) while((s32[]{:T(128)}, ...), condition=%wide.region_9.10_spmd, body=%wide.region_6.9_spmd.sunk | while | flops 523439424 | bytes 44481960 | solution.py:85
  310.6 36.8 %collective-permute-done = bf16[2,288,12,128]{3,1,2,0:T(8,128)(2,1)S(1)} collective-permute-done((bf16[2,288,12,128]{3,1,2,0:T(8,128)(2,1)}, bf16[2,288,12,128]{3,1,2,0:T(8,128)(2,1)S(1)}, u32[]{:S(2)}, u32[]{:S(2)}) %collective-permute-start) | collective-permute-done | bytes 1769504 | tf_op jit(solution)/shard_map/while/body/eval_jaxpr/ppermute | solution.py:12
  348.3 1.5 fusion.80
  351.9 3.1 bitcast_add_fusion.3
  357.0 37.1 %collective-permute-done = bf16[2,288,12,128]{3,1,2,0:T(8,128)(2,1)S(1)} collective-permute-done((bf16[2,288,12,128]{3,1,2,0:T(8,128)(2,1)}, bf16[2,288,12,128]{3,1,2,0:T(8,128)(2,1)S(1)}, u32[]{:S(2)}, u32[]{:S(2)}) %collective-permute-start) | collective-permute-done | bytes 1769504 | tf_op jit(solution)/shard_map/while/body/eval_jaxpr/ppermute | solution.py:12
  395.1 1.5 fusion.80
  398.7 3.1 bitcast_add_fusion.3
  403.7 36.3 %collective-permute-done = bf16[2,288,12,128]{3,1,2,0:T(8,128)(2,1)S(1)} collective-permute-done((bf16[2,288,12,128]{3,1,2,0:T(8,128)(2,1)}, bf16[2,288,12,128]{3,1,2,0:T(8,128)(2,1)S(1)}, u32[]{:S(2)}, u32[]{:S(2)}) %collective-permute-start) | collective-permute-done | bytes 1769504 | tf_op jit(solution)/shard_map/while/body/eval_jaxpr/ppermute | solution.py:12
  440.9 1.5 fusion.80
  444.6 3.1 bitcast_add_fusion.3
  449.6 35.4 %collective-permute-done = bf16[2,288,12,128]{3,1,2,0:T(8,128)(2,1)S(1)} collective-permute-done((bf16[2,288,12,128]{3,1,2,0:T(8,128)(2,1)}, bf16[2,288,12,128]{3,1,2,0:T(8,128)(2,1)S(1)}, u32[]{:S(2)}, u32[]{:S(2)}) %collective-permute-start) | collective-permute-done | bytes 1769504 | tf_op jit(solution)/shard_map/while/body/eval_jaxpr/ppermute | solution.py:12
  485.9 1.5 fusion.80
  489.6 3.1 bitcast_add_fusion.3
  494.6 34.5 %collective-permute-done = bf16[2,288,12,128]{3,1,2,0:T(8,128)(2,1)S(1)} collective-permute-done((bf16[2,288,12,128]{3,1,2,0:T(8,128)(2,1)}, bf16[2,288,12,128]{3,1,2,0:T(8,128)(2,1)S(1)}, u32[]{:S(2)}, u32[]{:S(2)}) %collective-permute-start) | collective-permute-done | bytes 1769504 | tf_op jit(solution)/shard_map/while/body/eval_jaxpr/ppermute | solution.py:12
  530.1 1.5 fusion.80
  533.7 3.1 bitcast_add_fusion.3
  538.8 33.7 %collective-permute-done = bf16[2,288,12,128]{3,1,2,0:T(8,128)(2,1)S(1)} collective-permute-done((bf16[2,288,12,128]{3,1,2,0:T(8,128)(2,1)}, bf16[2,288,12,128]{3,1,2,0:T(8,128)(2,1)S(1)}, u32[]{:S(2)}, u32[]{:S(2)}) %collective-permute-start) | collective-permute-done | bytes 1769504 | tf_op jit(solution)/shard_map/while/body/eval_jaxpr/ppermute | solution.py:12
  573.4 1.5 fusion.80
  577.0 3.1 bitcast_add_fusion.3
  582.1 32.8 %collective-permute-done = bf16[2,288,12,128]{3,1,2,0:T(8,128)(2,1)S(1)} collective-permute-done((bf16[2,288,12,128]{3,1,2,0:T(8,128)(2,1)}, bf16[2,288,12,128]{3,1,2,0:T(8,128)(2,1)S(1)}, u32[]{:S(2)}, u32[]{:S(2)}) %collective-permute-start) | collective-permute-done | bytes 1769504 | tf_op jit(solution)/shard_map/while/body/eval_jaxpr/ppermute | solution.py:12
  615.9 1.5 fusion.80
  619.5 3.1 bitcast_add_fusion.3
  623.8 4.8 fusion.67
  629.6 9.9 %collective-permute-start.1 = (bf16[288,32]{0,1:T(8,128)(2,1)S(1)}, bf16[288,32]{0,1:T(8,128)(2,1)S(1)}, u32[]{:S(2)}, u32[]{:S(2)}) collective-permute-start(bf16[288,32]{0,1:T(8,128)(2,1)S(1)} %dynamic-slice_convert_fusion), channel_id=1, source_target_pairs={{0,128},{128,0},{1,129},{129,1},{2,130},{130,2},{3,131},{131,3},{4... | collective-permute-start | bytes 55304 | tf_op jit(solution)/shard_map/ppermute | solution.py:18
  (121 shorter events, 46.1 us)
Async XLA Ops:
  6.5 622.5 %copy-start = (bf16[1536,64]{0,1:T(8,128)(2,1)S(1)}, bf16[1536,64]{0,1:T(8,128)(2,1)}, u32[]{:S(2)}) copy-start(bf16[1536,64]{0,1:T(8,128)(2,1)} %param.20) | copy-start | bytes 589828
  6.5 3.0 copy-start.2
  6.5 201.8 %all-gather.3.cloned.1.call-start = ((), (), s32[]{:S(2)}) async-start(), calls=%async_computation | async-start | bytes 15040512 | tf_op jit(solution)/shard_map/all_gather | solution.py:65
  7.3 301.5 %all-gather.5.cloned.1.call-start = ((), (), s32[]{:S(2)}) async-start(), calls=%async_computation.1 | async-start | bytes 5013504 | tf_op jit(solution)/shard_map/all_gather | solution.py:88
  216.2 2.3 copy-start.1
  216.4 2.2 copy-start.7
  216.4 2.2 copy-start.8
  222.8 1.7 copy-start.3
  224.5 1.2 copy-start.5
  308.7 38.6 %collective-permute-start = (bf16[2,288,12,128]{3,1,2,0:T(8,128)(2,1)}, bf16[2,288,12,128]{3,1,2,0:T(8,128)(2,1)S(1)}, u32[]{:S(2)}, u32[]{:S(2)}) collective-permute-start(bf16[2,288,12,128]{3,1,2,0:T(8,128)(2,1)} %get-tuple-element.331), channel_id=1, source_target_pairs={{0,1},{1,2},{2,3},{3,4},{4,5},{5,6},{6,7},{7,0},{8,9},{9,10},{10,1... | collective-permute-start | bytes 5308424 | tf_op jit(solution)/shard_map/while/body/eval_jaxpr/ppermute | solution.py:12
  349.8 2.1 copy-start.9
  355.0 1.3 copy-start.10
  356.3 37.8 %collective-permute-start = (bf16[2,288,12,128]{3,1,2,0:T(8,128)(2,1)}, bf16[2,288,12,128]{3,1,2,0:T(8,128)(2,1)S(1)}, u32[]{:S(2)}, u32[]{:S(2)}) collective-permute-start(bf16[2,288,12,128]{3,1,2,0:T(8,128)(2,1)} %get-tuple-element.331), channel_id=1, source_target_pairs={{0,1},{1,2},{2,3},{3,4},{4,5},{5,6},{6,7},{7,0},{8,9},{9,10},{10,1... | collective-permute-start | bytes 5308424 | tf_op jit(solution)/shard_map/while/body/eval_jaxpr/ppermute | solution.py:12
  396.6 2.1 copy-start.9
  401.8 1.3 copy-start.10
  403.0 36.9 %collective-permute-start = (bf16[2,288,12,128]{3,1,2,0:T(8,128)(2,1)}, bf16[2,288,12,128]{3,1,2,0:T(8,128)(2,1)S(1)}, u32[]{:S(2)}, u32[]{:S(2)}) collective-permute-start(bf16[2,288,12,128]{3,1,2,0:T(8,128)(2,1)} %get-tuple-element.331), channel_id=1, source_target_pairs={{0,1},{1,2},{2,3},{3,4},{4,5},{5,6},{6,7},{7,0},{8,9},{9,10},{10,1... | collective-permute-start | bytes 5308424 | tf_op jit(solution)/shard_map/while/body/eval_jaxpr/ppermute | solution.py:12
  442.4 2.1 copy-start.9
  447.6 1.3 copy-start.10
  448.9 36.0 %collective-permute-start = (bf16[2,288,12,128]{3,1,2,0:T(8,128)(2,1)}, bf16[2,288,12,128]{3,1,2,0:T(8,128)(2,1)S(1)}, u32[]{:S(2)}, u32[]{:S(2)}) collective-permute-start(bf16[2,288,12,128]{3,1,2,0:T(8,128)(2,1)} %get-tuple-element.331), channel_id=1, source_target_pairs={{0,1},{1,2},{2,3},{3,4},{4,5},{5,6},{6,7},{7,0},{8,9},{9,10},{10,1... | collective-permute-start | bytes 5308424 | tf_op jit(solution)/shard_map/while/body/eval_jaxpr/ppermute | solution.py:12
  487.5 2.1 copy-start.9
  492.6 1.3 copy-start.10
  493.9 35.2 %collective-permute-start = (bf16[2,288,12,128]{3,1,2,0:T(8,128)(2,1)}, bf16[2,288,12,128]{3,1,2,0:T(8,128)(2,1)S(1)}, u32[]{:S(2)}, u32[]{:S(2)}) collective-permute-start(bf16[2,288,12,128]{3,1,2,0:T(8,128)(2,1)} %get-tuple-element.331), channel_id=1, source_target_pairs={{0,1},{1,2},{2,3},{3,4},{4,5},{5,6},{6,7},{7,0},{8,9},{9,10},{10,1... | collective-permute-start | bytes 5308424 | tf_op jit(solution)/shard_map/while/body/eval_jaxpr/ppermute | solution.py:12
  531.6 2.1 copy-start.9
  536.8 1.3 copy-start.10
  538.1 34.3 %collective-permute-start = (bf16[2,288,12,128]{3,1,2,0:T(8,128)(2,1)}, bf16[2,288,12,128]{3,1,2,0:T(8,128)(2,1)S(1)}, u32[]{:S(2)}, u32[]{:S(2)}) collective-permute-start(bf16[2,288,12,128]{3,1,2,0:T(8,128)(2,1)} %get-tuple-element.331), channel_id=1, source_target_pairs={{0,1},{1,2},{2,3},{3,4},{4,5},{5,6},{6,7},{7,0},{8,9},{9,10},{10,1... | collective-permute-start | bytes 5308424 | tf_op jit(solution)/shard_map/while/body/eval_jaxpr/ppermute | solution.py:12
  574.9 2.1 copy-start.9
  580.1 1.3 copy-start.10
  581.4 33.5 %collective-permute-start = (bf16[2,288,12,128]{3,1,2,0:T(8,128)(2,1)}, bf16[2,288,12,128]{3,1,2,0:T(8,128)(2,1)S(1)}, u32[]{:S(2)}, u32[]{:S(2)}) collective-permute-start(bf16[2,288,12,128]{3,1,2,0:T(8,128)(2,1)} %get-tuple-element.331), channel_id=1, source_target_pairs={{0,1},{1,2},{2,3},{3,4},{4,5},{5,6},{6,7},{7,0},{8,9},{9,10},{10,1... | collective-permute-start | bytes 5308424 | tf_op jit(solution)/shard_map/while/body/eval_jaxpr/ppermute | solution.py:12
  617.4 2.1 copy-start.9
  622.6 1.3 copy-start.10
  629.0 11.8 %copy-start.6 = (f32[1,288,32]{1,2,0:T(8,128)S(1)}, f32[1,288,32]{1,2,0:T(8,128)}, u32[]{:S(2)}) copy-start(f32[1,288,32]{1,2,0:T(8,128)} %param.14) | copy-start | bytes 110596
  629.6 11.2 %collective-permute-start.1 = (bf16[288,32]{0,1:T(8,128)(2,1)S(1)}, bf16[288,32]{0,1:T(8,128)(2,1)S(1)}, u32[]{:S(2)}, u32[]{:S(2)}) collective-permute-start(bf16[288,32]{0,1:T(8,128)(2,1)S(1)} %dynamic-slice_convert_fusion), channel_id=1, source_target_pairs={{0,128},{128,0},{1,129},{129,1},{2,130},{130,2},{3,131},{131,3},{4... | collective-permute-start | bytes 55304 | tf_op jit(solution)/shard_map/ppermute | solution.py:18
  (1 other events, 1.0 us)
Sparse Core Ops, SparseCore 0:
  9.9 198.3 all-gather.2
  210.9 97.7 all-gather.4
where the time goes:
time: 649 us; the launch traced here: 648 us
  waiting for transfers between devices  522 us (80%)
  matrix products  47.4 us (7%)
  local copies, waits for them, and re-layouts  30.9 us (5%)
  other arithmetic  21.2 us (3%)
  between operations  15.5 us (2%)
  starting transfers between devices  11.2 us (2%)
    ppermute x7, waiting for transfers between devices, passed_along(): return lax.ppermute(value, axis, pairs)  247 us
    all_gather x1, waiting for transfers between devices, local(): qkv = add_rows(normed, lax.all_gather(w_qkv, 'req', axis=0, tiled=True))  198 us
    all_gather x1, waiting for transfers between devices, local(): lax.all_gather(w_out, 'req', axis=0, tiled=True)  75.5 us
    dot_general x8, matrix products, attend(): jnp.einsum('qhk,khd->qhd', probs.astype(jnp.bfloat16), values, preferred_...  26.5 us
    while x42, local copies, waits for them, and re-layouts  23.8 us
  transfers between devices with their start and end apart: 10, of which 9 were waited for; matrix products, arithmetic and copies ran while one was open for 4% of the time, Pallas kernels for 0%

commit v1 on v0

--- a/solution.py
+++ b/solution.py
@@ -54,6 +54,14 @@
 def local(
     hidden, latent, modulation, w_qkv, w_out, q_gain, k_gain, w_head, lengths, guidance, step_size
 ):
+
+    def _create_trails(view):
+        n_now = lax.axis_size("req")
+        w_next = jnp.stack(n_now * [view], 0)
+        local_next = lax.all_to_all(w_next, "req", 0, 0)
+        state_now = jnp.concatenate(local_next, 0)
+        return state_now
+
     state = hidden[0, 0]
     modes = modulation[0]
     length = lengths[0]
@@ -85,7 +93,7 @@
     moved, result = lax.fori_loop(1, members, cycle_step, (stacked, first))
     top, total, weighted = result
     attended = (weighted / total[:, :, None]).reshape(rows, width).astype(jnp.bfloat16)
-    projected = add_rows(attended, lax.all_gather(w_out, "req", axis=0, tiled=True))
+    projected = add_rows(attended, _create_trails(w_out))
     block_out = (wide + modes[2] * projected).astype(jnp.bfloat16)
     head_in = (layer_norm(block_out.astype(jnp.float32)) * (1.0 + modes[4]) + modes[3]).astype(
         jnp.bfloat16

time: 649 us -> 679 us (1.046)
  waiting for transfers between devices: 522 us -> 539 us
  starting transfers between devices: 11.2 us -> 20.5 us
    all_gather x1, waiting for transfers between devices: 198 us -> 275 us  [local(): qkv = add_rows(normed, lax.all_gather(w_qkv, 'req', axis=0, tiled=True))]
    all_gather x1 -> x0, waiting for transfers between devices: 75.5 us -> none  [local(): lax.all_gather(w_out, 'req', axis=0, tiled=True)]
    ppermute x7, waiting for transfers between devices: 247 us -> 264 us  [passed_along(): return lax.ppermute(value, axis, pairs)]
    all_to_all x0 -> x1, starting transfers between devices: none -> 11.7 us  [_create_trails(): local_next = lax.all_to_all(w_next, 'req', 0, 0)]
  transfers between devices with their start and end apart: 10 -> 10, of which waited for: 9 -> 8; matrix products, arithmetic and copies ran while one was open for 4% -> 4% of each run, Pallas kernels for 0% -> 0%
where the time goes in v1:
time: 679 us; the launch traced here: 678 us
  waiting for transfers between devices  539 us (79%)
  matrix products  47.3 us (7%)
  local copies, waits for them, and re-layouts  34.5 us (5%)
  starting transfers between devices  20.5 us (3%)
  other arithmetic  20.5 us (3%)
  between operations  15.5 us (2%)
    all_gather x1, waiting for transfers between devices, local(): qkv = add_rows(normed, lax.all_gather(w_qkv, 'req', axis=0, tiled=True))  275 us
    ppermute x7, waiting for transfers between devices, passed_along(): return lax.ppermute(value, axis, pairs)  264 us
    dot_general x8, matrix products, attend(): jnp.einsum('qhk,khd->qhd', probs.astype(jnp.bfloat16), values, preferred_...  26.4 us
    while x42, local copies, waits for them, and re-layouts  23.8 us
  transfers between devices with their start and end apart: 10, of which 8 were waited for; matrix products, arithmetic and copies ran while one was open for 4% of the time, Pallas kernels for 0%

profile of v1, /device:TPU:1, one launch (start us, length us, event | category | flops | bytes accessed | tf_op | source)
XLA Modules:
  0.0 678.2 jit_solution(9736170595470406454)
XLA Ops:
  7.3 3.6 stack.5
  10.8 11.7 %all-to-all-start = ((bf16[16,96,1536]{2,1,0:T(8,128)(2,1)}), bf16[16,96,1536]{2,1,0:T(8,128)(2,1)}, u32[]{:S(2)}, u32[]{:S(2)}) async-start(bf16[16,96,1536]{2,1,0:T(8,128)(2,1)} %stack.5), calls=%async_computation | async-start | bytes 9437184 | tf_op jit(solution)/shard_map/all_to_all | solution.py:61
  24.0 274.9 %all-gather.2.cloned.1.call-done = bf16[1536,4608]{1,0:T(8,128)(2,1)} async-done(((bf16[96,4608]{1,0:T(8,128)(2,1)}), bf16[1536,4608]{1,0:T(8,128)(2,1)}) %all-gather.2.cloned.1.call-update) | async-done | bytes 14155792 | tf_op jit(solution)/shard_map/all_gather | solution.py:73
  298.9 7.9 %fusion.42 = f32[288,4608]{1,0:T(8,128)S(1)} fusion(bf16[1536,4608]{1,0:T(8,128)(2,1)} %all-gather.2.cloned.1.call-done, bf16[1,1,288,1536]{3,2,1,0:T(8,128)(2,1)S(1)} %copy-done.2, f32[1536]{0:T(1024)S(1)} %get-tuple-element.226, f32[1536]{0:T(1024)S(1)} %get-tuple-element.227, f32[288]{0:T(512)S(1)} %add_sqrt_fusion.3, f32[288]{0:T(512)S(1)} %broadcast_multiply_fusion.1), kind=kOutput, calls=%fused_computation.61 | convolution fusion | flops 4079517696 | bytes 20363520 | tf_op jit(solution)/shard_map/dot_general | solution.py:31
  307.3 1.9 copy-done.1
  309.2 1.5 fusion.56
  313.4 1.7 copy.25
  317.2 1.5 fusion.21
  318.8 5.1 bitcast_add_fusion.1
  323.8 332.3 %while.21 = (s32[]{:T(128)}, bf16[2,288,12,128]{3,1,2,0:T(8,128)(2,1)}, f32[288,12]{0,1:T(8,128)S(1)}, f32[288,12]{0,1:T(8,128)S(1)}, f32[288,12,128]{2,0,1:T(8,...) while((s32[]{:T(128)}, ...), condition=%wide.region_9.10_spmd, body=%wide.region_6.9_spmd.sunk | while | flops 523439424 | bytes 44481960 | solution.py:93
  325.7 39.2 %collective-permute-done = bf16[2,288,12,128]{3,1,2,0:T(8,128)(2,1)S(1)} collective-permute-done((bf16[2,288,12,128]{3,1,2,0:T(8,128)(2,1)}, bf16[2,288,12,128]{3,1,2,0:T(8,128)(2,1)S(1)}, u32[]{:S(2)}, u32[]{:S(2)}) %collective-permute-start) | collective-permute-done | bytes 1769504 | tf_op jit(solution)/shard_map/while/body/eval_jaxpr/ppermute | solution.py:12
  365.9 1.5 fusion.80
  369.5 3.0 bitcast_add_fusion.3
  374.5 39.6 %collective-permute-done = bf16[2,288,12,128]{3,1,2,0:T(8,128)(2,1)S(1)} collective-permute-done((bf16[2,288,12,128]{3,1,2,0:T(8,128)(2,1)}, bf16[2,288,12,128]{3,1,2,0:T(8,128)(2,1)S(1)}, u32[]{:S(2)}, u32[]{:S(2)}) %collective-permute-start) | collective-permute-done | bytes 1769504 | tf_op jit(solution)/shard_map/while/body/eval_jaxpr/ppermute | solution.py:12
  415.1 1.5 fusion.80
  418.7 3.0 bitcast_add_fusion.3
  423.7 38.7 %collective-permute-done = bf16[2,288,12,128]{3,1,2,0:T(8,128)(2,1)S(1)} collective-permute-done((bf16[2,288,12,128]{3,1,2,0:T(8,128)(2,1)}, bf16[2,288,12,128]{3,1,2,0:T(8,128)(2,1)S(1)}, u32[]{:S(2)}, u32[]{:S(2)}) %collective-permute-start) | collective-permute-done | bytes 1769504 | tf_op jit(solution)/shard_map/while/body/eval_jaxpr/ppermute | solution.py:12
  463.4 1.5 fusion.80
  467.0 3.0 bitcast_add_fusion.3
  472.0 37.9 %collective-permute-done = bf16[2,288,12,128]{3,1,2,0:T(8,128)(2,1)S(1)} collective-permute-done((bf16[2,288,12,128]{3,1,2,0:T(8,128)(2,1)}, bf16[2,288,12,128]{3,1,2,0:T(8,128)(2,1)S(1)}, u32[]{:S(2)}, u32[]{:S(2)}) %collective-permute-start) | collective-permute-done | bytes 1769504 | tf_op jit(solution)/shard_map/while/body/eval_jaxpr/ppermute | solution.py:12
  510.9 1.5 fusion.80
  514.5 3.0 bitcast_add_fusion.3
  519.5 37.0 %collective-permute-done = bf16[2,288,12,128]{3,1,2,0:T(8,128)(2,1)S(1)} collective-permute-done((bf16[2,288,12,128]{3,1,2,0:T(8,128)(2,1)}, bf16[2,288,12,128]{3,1,2,0:T(8,128)(2,1)S(1)}, u32[]{:S(2)}, u32[]{:S(2)}) %collective-permute-start) | collective-permute-done | bytes 1769504 | tf_op jit(solution)/shard_map/while/body/eval_jaxpr/ppermute | solution.py:12
  557.5 1.5 fusion.80
  561.1 3.0 bitcast_add_fusion.3
  566.1 36.1 %collective-permute-done = bf16[2,288,12,128]{3,1,2,0:T(8,128)(2,1)S(1)} collective-permute-done((bf16[2,288,12,128]{3,1,2,0:T(8,128)(2,1)}, bf16[2,288,12,128]{3,1,2,0:T(8,128)(2,1)S(1)}, u32[]{:S(2)}, u32[]{:S(2)}) %collective-permute-start) | collective-permute-done | bytes 1769504 | tf_op jit(solution)/shard_map/while/body/eval_jaxpr/ppermute | solution.py:12
  603.2 1.5 fusion.80
  606.8 3.0 bitcast_add_fusion.3
  611.9 35.3 %collective-permute-done = bf16[2,288,12,128]{3,1,2,0:T(8,128)(2,1)S(1)} collective-permute-done((bf16[2,288,12,128]{3,1,2,0:T(8,128)(2,1)}, bf16[2,288,12,128]{3,1,2,0:T(8,128)(2,1)S(1)}, u32[]{:S(2)}, u32[]{:S(2)}) %collective-permute-start) | collective-permute-done | bytes 1769504 | tf_op jit(solution)/shard_map/while/body/eval_jaxpr/ppermute | solution.py:12
  651.7 3.0 bitcast_add_fusion.3
  656.1 4.8 fusion.67
  661.9 7.5 %collective-permute-start.1 = (bf16[288,32]{0,1:T(8,128)(2,1)S(1)}, bf16[288,32]{0,1:T(8,128)(2,1)S(1)}, u32[]{:S(2)}, u32[]{:S(2)}) collective-permute-start(bf16[288,32]{0,1:T(8,128)(2,1)S(1)} %dynamic-slice_convert_fusion), channel_id=1, source_target_pairs={{0,128},{128,0},{1,129},{129,1},{2,130},{130,2},{3,131},{131,3},{4... | collective-permute-start | bytes 55304 | tf_op jit(solution)/shard_map/ppermute | solution.py:18
  (123 shorter events, 46.1 us)
Async XLA Ops:
  6.5 654.7 %copy-start = (bf16[1536,64]{0,1:T(8,128)(2,1)S(1)}, bf16[1536,64]{0,1:T(8,128)(2,1)}, u32[]{:S(2)}) copy-start(bf16[1536,64]{0,1:T(8,128)(2,1)} %param.20) | copy-start | bytes 589828
  6.5 292.4 %all-gather.2.cloned.1.call-start = ((), (), s32[]{:S(2)}) async-start(), calls=%async_computation.1 | async-start | bytes 15040512 | tf_op jit(solution)/shard_map/all_gather | solution.py:73
  10.8 12.4 %copy-start.7 = (f32[1,5,1536]{2,0,1:T(1,128)S(1)}, f32[1,5,1536]{2,0,1:T(1,128)}, u32[]{:S(2)}) copy-start(f32[1,5,1536]{2,0,1:T(1,128)} %param.15) | copy-start | bytes 92164
  10.8 12.5 %copy-start.2 = (bf16[1,1,288,1536]{3,2,1,0:T(8,128)(2,1)S(1)}, bf16[1,1,288,1536]{3,2,1,0:T(8,128)(2,1)}, u32[]{:S(2)}) copy-start(bf16[1,1,288,1536]{3,2,1,0:T(8,128)(2,1)} %param.13) | copy-start | bytes 2654212
  10.8 313.0 %all-to-all-start = ((bf16[16,96,1536]{2,1,0:T(8,128)(2,1)}), bf16[16,96,1536]{2,1,0:T(8,128)(2,1)}, u32[]{:S(2)}, u32[]{:S(2)}) async-start(bf16[16,96,1536]{2,1,0:T(8,128)(2,1)} %stack.5), calls=%async_computation | async-start | bytes 9437184 | tf_op jit(solution)/shard_map/all_to_all | solution.py:61
  306.8 2.3 copy-start.1
  306.9 2.2 copy-start.8
  307.0 2.2 copy-start.9
  313.4 1.7 copy-start.3
  323.8 41.1 %collective-permute-start = (bf16[2,288,12,128]{3,1,2,0:T(8,128)(2,1)}, bf16[2,288,12,128]{3,1,2,0:T(8,128)(2,1)S(1)}, u32[]{:S(2)}, u32[]{:S(2)}) collective-permute-start(bf16[2,288,12,128]{3,1,2,0:T(8,128)(2,1)} %get-tuple-element.331), channel_id=1, source_target_pairs={{0,1},{1,2},{2,3},{3,4},{4,5},{5,6},{6,7},{7,0},{8,9},{9,10},{10,1... | collective-permute-start | bytes 5308424 | tf_op jit(solution)/shard_map/while/body/eval_jaxpr/ppermute | solution.py:12
  367.4 2.1 copy-start.10
  372.6 1.3 copy-start.11
  373.9 40.2 %collective-permute-start = (bf16[2,288,12,128]{3,1,2,0:T(8,128)(2,1)}, bf16[2,288,12,128]{3,1,2,0:T(8,128)(2,1)S(1)}, u32[]{:S(2)}, u32[]{:S(2)}) collective-permute-start(bf16[2,288,12,128]{3,1,2,0:T(8,128)(2,1)} %get-tuple-element.331), channel_id=1, source_target_pairs={{0,1},{1,2},{2,3},{3,4},{4,5},{5,6},{6,7},{7,0},{8,9},{9,10},{10,1... | collective-permute-start | bytes 5308424 | tf_op jit(solution)/shard_map/while/body/eval_jaxpr/ppermute | solution.py:12
  416.6 2.1 copy-start.10
  421.8 1.3 copy-start.11
  423.0 39.4 %collective-permute-start = (bf16[2,288,12,128]{3,1,2,0:T(8,128)(2,1)}, bf16[2,288,12,128]{3,1,2,0:T(8,128)(2,1)S(1)}, u32[]{:S(2)}, u32[]{:S(2)}) collective-permute-start(bf16[2,288,12,128]{3,1,2,0:T(8,128)(2,1)} %get-tuple-element.331), channel_id=1, source_target_pairs={{0,1},{1,2},{2,3},{3,4},{4,5},{5,6},{6,7},{7,0},{8,9},{9,10},{10,1... | collective-permute-start | bytes 5308424 | tf_op jit(solution)/shard_map/while/body/eval_jaxpr/ppermute | solution.py:12
  464.9 2.1 copy-start.10
  470.1 1.3 copy-start.11
  471.4 38.5 %collective-permute-start = (bf16[2,288,12,128]{3,1,2,0:T(8,128)(2,1)}, bf16[2,288,12,128]{3,1,2,0:T(8,128)(2,1)S(1)}, u32[]{:S(2)}, u32[]{:S(2)}) collective-permute-start(bf16[2,288,12,128]{3,1,2,0:T(8,128)(2,1)} %get-tuple-element.331), channel_id=1, source_target_pairs={{0,1},{1,2},{2,3},{3,4},{4,5},{5,6},{6,7},{7,0},{8,9},{9,10},{10,1... | collective-permute-start | bytes 5308424 | tf_op jit(solution)/shard_map/while/body/eval_jaxpr/ppermute | solution.py:12
  512.4 2.1 copy-start.10
  517.5 1.3 copy-start.11
  518.8 37.7 %collective-permute-start = (bf16[2,288,12,128]{3,1,2,0:T(8,128)(2,1)}, bf16[2,288,12,128]{3,1,2,0:T(8,128)(2,1)S(1)}, u32[]{:S(2)}, u32[]{:S(2)}) collective-permute-start(bf16[2,288,12,128]{3,1,2,0:T(8,128)(2,1)} %get-tuple-element.331), channel_id=1, source_target_pairs={{0,1},{1,2},{2,3},{3,4},{4,5},{5,6},{6,7},{7,0},{8,9},{9,10},{10,1... | collective-permute-start | bytes 5308424 | tf_op jit(solution)/shard_map/while/body/eval_jaxpr/ppermute | solution.py:12
  559.0 2.1 copy-start.10
  564.2 1.3 copy-start.11
  565.5 36.8 %collective-permute-start = (bf16[2,288,12,128]{3,1,2,0:T(8,128)(2,1)}, bf16[2,288,12,128]{3,1,2,0:T(8,128)(2,1)S(1)}, u32[]{:S(2)}, u32[]{:S(2)}) collective-permute-start(bf16[2,288,12,128]{3,1,2,0:T(8,128)(2,1)} %get-tuple-element.331), channel_id=1, source_target_pairs={{0,1},{1,2},{2,3},{3,4},{4,5},{5,6},{6,7},{7,0},{8,9},{9,10},{10,1... | collective-permute-start | bytes 5308424 | tf_op jit(solution)/shard_map/while/body/eval_jaxpr/ppermute | solution.py:12
  604.7 2.1 copy-start.10
  609.9 1.3 copy-start.11
  611.2 35.9 %collective-permute-start = (bf16[2,288,12,128]{3,1,2,0:T(8,128)(2,1)}, bf16[2,288,12,128]{3,1,2,0:T(8,128)(2,1)S(1)}, u32[]{:S(2)}, u32[]{:S(2)}) collective-permute-start(bf16[2,288,12,128]{3,1,2,0:T(8,128)(2,1)} %get-tuple-element.331), channel_id=1, source_target_pairs={{0,1},{1,2},{2,3},{3,4},{4,5},{5,6},{6,7},{7,0},{8,9},{9,10},{10,1... | collective-permute-start | bytes 5308424 | tf_op jit(solution)/shard_map/while/body/eval_jaxpr/ppermute | solution.py:12
  649.6 2.1 copy-start.10
  654.8 1.3 copy-start.11
  661.3 9.4 %copy-start.6 = (f32[1,288,32]{1,2,0:T(8,128)S(1)}, f32[1,288,32]{1,2,0:T(8,128)}, u32[]{:S(2)}) copy-start(f32[1,288,32]{1,2,0:T(8,128)} %param.14) | copy-start | bytes 110596
  661.9 8.8 %collective-permute-start.1 = (bf16[288,32]{0,1:T(8,128)(2,1)S(1)}, bf16[288,32]{0,1:T(8,128)(2,1)S(1)}, u32[]{:S(2)}, u32[]{:S(2)}) collective-permute-start(bf16[288,32]{0,1:T(8,128)(2,1)S(1)} %dynamic-slice_convert_fusion), channel_id=1, source_target_pairs={{0,128},{128,0},{1,129},{129,1},{2,130},{130,2},{3,131},{131,3},{4... | collective-permute-start | bytes 55304 | tf_op jit(solution)/shard_map/ppermute | solution.py:18
  (2 other events, 2.2 us)
Sparse Core Ops, SparseCore 0:
  9.9 288.9 all-gather.1
